TPU v7x, 32 devices: a whole 2x2x4 slice. The times are simulated.
32 devices in a mesh: dp: 8 (over z, x), tensor: 4 (over y, core).
Axes of the slice: x: 2, y: 2, z: 4, core: 2. Of those that a mesh axis runs over, the one named last changes fastest.
Arguments:
- inputs: bfloat16 [8192, 4096], P('dp'), may hold values from -6 to 6
- out_grads: bfloat16 [8192, 6144], P('dp', 'tensor'), may hold values from -0.01953125 to 0.01953125
- left_factor: float32 [4096, 4096], P('dp', 'tensor'), may hold values from -6 to 6
- right_factor: float32 [6144, 6144], P('dp', 'tensor'), may hold values from -6 to 6
- left_basis: float32 [4096, 4096], P('dp', 'tensor'), may hold values from -0.09375 to 0.09375
- right_basis: float32 [6144, 6144], P('dp', 'tensor'), may hold values from -0.078125 to 0.078125
Outputs:
- left_new: float32 [4096, 4096], P('dp', 'tensor')
- right_new: float32 [6144, 6144], P('dp', 'tensor')
- rotated: float32 [4096, 6144], P('dp', 'tensor')
All inputs are finite; a program needn't handle non-finite values.
Results may differ from a plain program's by a relative error of at most 0.019.
Values may be sent and summed in bfloat16 or wider, within the bound.
A program may use at most 192 MiB of HBM per device.

v0:
```python
import jax
import jax.numpy as jnp
from jax import lax
from jax.sharding import PartitionSpec as P


def shards(inputs, out_grads, left_factor, right_factor, left_basis, right_basis):
    krows = left_factor.shape[0]
    mrows = right_factor.shape[0]
    mcols = out_grads.shape[1]
    right_low = right_basis.astype(jnp.bfloat16)
    left_low = left_basis.astype(jnp.bfloat16)
    summed = lax.psum_scatter(
        lax.dot_general(
            inputs, out_grads, (((0,), (0,)), ((), ())), preferred_element_type=jnp.float32
        ).astype(jnp.bfloat16),
        "dp",
        scatter_dimension=0,
        tiled=True,
    )
    col_panel, basis_panel = (
        lax.all_gather(summed, "dp", axis=0, tiled=True),
        lax.all_gather(right_low, "dp", axis=0, tiled=True),
    )
    row_panel, left_rows = (
        lax.all_gather(summed, "tensor", axis=1, tiled=True),
        lax.all_gather(left_low, "tensor", axis=1, tiled=True),
    )
    gram_left = lax.psum_scatter(
        lax.dot_general(
            col_panel, summed, (((1,), (1,)), ((), ())), preferred_element_type=jnp.float32
        ).astype(jnp.bfloat16),
        "tensor",
        scatter_dimension=0,
        tiled=True,
    ).astype(jnp.float32)
    left_new = 0.95 * left_factor + 0.05 * gram_left.T
    turned = jnp.dot(row_panel, basis_panel, preferred_element_type=jnp.float32).astype(
        jnp.bfloat16
    )
    stride = mrows + krows
    blocks = lax.axis_size("dp") * stride // stride
    right_part = lax.dot_general(
        row_panel, summed, (((0,), (0,)), ((), ())), preferred_element_type=jnp.float32
    )
    rot_part = lax.dot_general(
        left_rows, turned, (((0,), (0,)), ((), ())), preferred_element_type=jnp.float32
    )
    joined = jnp.concatenate(
        [right_part.reshape(blocks, mrows, mcols), rot_part.reshape(blocks, krows, mcols)], axis=1
    )
    together = lax.psum_scatter(
        joined.reshape(blocks * stride, mcols).astype(jnp.bfloat16),
        "dp",
        scatter_dimension=0,
        tiled=True,
    ).astype(jnp.float32)
    right_new = 0.95 * right_factor + 0.05 * together[:mrows]
    rotated = together[mrows:]
    return (left_new, right_new, rotated)


def solution(mesh):
    return jax.shard_map(
        shards,
        mesh=mesh,
        in_specs=(
            P("dp", None),
            P("dp", "tensor"),
            P("dp", "tensor"),
            P("dp", "tensor"),
            P("dp", "tensor"),
            P("dp", "tensor"),
        ),
        out_specs=(P("dp", "tensor"), P("dp", "tensor"), P("dp", "tensor")),
        check_vma=False,
    )
```

profile of v0, /device:TPU:0, one launch (start us, length us, event | category | flops | bytes accessed | tf_op | source)
XLA Modules:
  0.0 1462.3 jit_solution(1834453289369584762)
XLA Ops:
  7.2 1.8 copy-done
  9.1 19.2 %convolution_convert_fusion.2 = bf16[4096,1536]{1,0:T(8,128)(2,1)} fusion(bf16[1024,4096]{1,0:T(8,128)(2,1)} %param.6, bf16[1024,1536]{1,0:T(8,128)(2,1)S(1)} %copy-done), kind=kOutput, calls=%fused_computation.3 | convolution fusion | flops 12891193344 | bytes 24117248 | tf_op jit(solution)/shard_map/dot_general | solution.py:14
  28.3 210.1 %reduce-scatter.4.cloned.1.call-done = bf16[512,1536]{1,0:T(8,128)(2,1)} async-done(((bf16[4096,1536]{1,0:T(8,128)(2,1)}), bf16[512,1536]{1,0:T(8,128)(2,1)}) %reduce-scatter.4.cloned.1.call-update) | async-done | bytes 1572880 | tf_op jit(solution)/shard_map/reduce_scatter | solution.py:13
  238.5 1.1 convert_element_type.30
  239.6 0.0 all-gather.9.cloned.1.call-start
  239.7 4.1 convert_element_type.28
  243.9 0.5 all-gather.7.cloned.1.call-update
  244.5 171.6 %all-gather.5.cloned.1.call-done = bf16[4096,1536]{1,0:T(8,128)(2,1)} async-done(((bf16[512,1536]{1,0:T(8,128)(2,1)}), bf16[4096,1536]{1,0:T(8,128)(2,1)}) %all-gather.5.cloned.1.call-update) | async-done | bytes 12582928 | tf_op jit(solution)/shard_map/all_gather | solution.py:22
  416.1 12.9 convolution_convert_fusion.3
  429.0 0.2 reduce-scatter.8.cloned.1.call-start
  429.2 21.7 %all-gather.11.cloned.1.call-done = bf16[512,4096]{1,0:T(8,128)(2,1)} async-done(((bf16[512,1024]{1,0:T(8,128)(2,1)}), bf16[512,4096]{1,0:T(8,128)(2,1)}) %all-gather.11.cloned.1.call-update) | async-done | bytes 4194320 | tf_op jit(solution)/shard_map/all_gather | solution.py:27
  451.0 364.5 %all-gather.9.cloned.1.call-done = bf16[6144,1536]{1,0:T(8,128)(2,1)} async-done(((bf16[768,1536]{1,0:T(8,128)(2,1)}), bf16[6144,1536]{1,0:T(8,128)(2,1)}) %all-gather.9.cloned.1.call-update) | async-done | bytes 18874384 | tf_op jit(solution)/shard_map/all_gather | solution.py:23
  815.4 47.8 %all-gather.7.cloned.1.call-done = bf16[512,6144]{1,0:T(8,128)(2,1)} async-done(((bf16[512,1536]{1,0:T(8,128)(2,1)}), bf16[512,6144]{1,0:T(8,128)(2,1)}) %all-gather.7.cloned.1.call-update) | async-done | bytes 6291472 | tf_op jit(solution)/shard_map/all_gather | solution.py:26
  863.2 32.4 %fusion = bf16[4096,1536]{0,1:T(8,128)(2,1)} fusion(bf16[512,4096]{1,0:T(8,128)(2,1)} %all-gather.11.cloned.1.call-done, bf16[512,6144]{1,0:T(8,128)(2,1)} %all-gather.7.cloned.1.call-done, bf16[6144,1536]{1,0:T(8,128)(2,1)} %all-gather.9.cloned.1.call-done), kind=kOutput, calls=%fused_computation.4 | convolution fusion | flops 16113205248 | bytes 41943040 | tf_op jit(solution)/shard_map/dot_general | solution.py:46
  895.6 16.6 %copy.12 = bf16[4096,1536]{1,0:T(8,128)(2,1)} copy(bf16[4096,1536]{0,1:T(8,128)(2,1)} %fusion) | data formatting | bytes 25165824 | tf_op jit(solution)/shard_map/reshape | solution.py:50
  912.2 15.9 %convolution_convert_fusion = bf16[6144,1536]{1,0:T(8,128)(2,1)} fusion(bf16[512,6144]{1,0:T(8,128)(2,1)} %all-gather.7.cloned.1.call-done, bf16[512,1536]{1,0:T(8,128)(2,1)S(1)} %copy-done.3), kind=kOutput, calls=%fused_computation.1 | convolution fusion | flops 9673113600 | bytes 26738688 | tf_op jit(solution)/shard_map/dot_general | solution.py:43
  928.1 21.8 %pad_maximum_fusion = bf16[8,1280,1536]{2,1,0:T(8,128)(2,1)} fusion(bf16[8,512,1536]{2,1,0:T(8,128)(2,1)} %bitcast.17, bf16[8,768,1536]{2,1,0:T(8,128)(2,1)} %bitcast.18), kind=kLoop, calls=%fused_computation | loop fusion | flops 62914560 | bytes 62914560 | tf_op jit(solution)/shard_map/concatenate | solution.py:49
  950.0 1.9 copy.9
  951.9 2.9 bitcast_add_fusion
  954.8 3.0 copy.11
  957.8 486.5 %reduce-scatter.8.cloned.1.call-done = bf16[1280,1536]{1,0:T(8,128)(2,1)} async-done(((bf16[10240,1536]{1,0:T(8,128)(2,1)}), bf16[1280,1536]{1,0:T(8,128)(2,1)}) %reduce-scatter.8.cloned.1.call-update) | async-done | bytes 3932176 | tf_op jit(solution)/shard_map/reduce_scatter | solution.py:52
  1444.3 3.2 convert_element_type.32
  1447.5 5.8 fusion.1
  1453.3 2.1 slice.9
  (21 shorter events, 0.3 us)
Async XLA Ops:
  7.2 1.9 copy-start
  7.2 231.2 %reduce-scatter.4.cloned.1.call-start = ((), (), s32[]{:S(2)}) async-start(), calls=%async_computation.3 | async-start | bytes 14155776 | tf_op jit(solution)/shard_map/reduce_scatter | solution.py:13
  28.2 210.2 %copy-start.4 = (f32[512,1024]{1,0:T(8,128)S(1)}, f32[512,1024]{1,0:T(8,128)}, u32[]{:S(2)}) copy-start(f32[512,1024]{1,0:T(8,128)} %param.10) | copy-start | bytes 6291460
  28.3 387.9 %all-gather.5.cloned.1.call-start = ((), (), s32[]{:S(2)}) async-start(), calls=%async_computation.4 | async-start | bytes 14155776 | tf_op jit(solution)/shard_map/all_gather | solution.py:22
  238.4 212.6 %all-gather.11.cloned.1.call-start = ((), (), s32[]{:S(2)}) async-start(), calls=%async_computation.8 | async-start | bytes 5242880 | tf_op jit(solution)/shard_map/all_gather | solution.py:27
  239.6 176.5 %copy-start.3 = (bf16[512,1536]{1,0:T(8,128)(2,1)S(1)}, bf16[512,1536]{1,0:T(8,128)(2,1)}, u32[]{:S(2)}) copy-start(bf16[512,1536]{1,0:T(8,128)(2,1)} %reduce-scatter.4.cloned.1.call-done) | copy-start | bytes 4718596
  239.6 575.8 %all-gather.9.cloned.1.call-start = ((), (), s32[]{:S(2)}) async-start(), calls=%async_computation.7 | async-start | bytes 21233664 | tf_op jit(solution)/shard_map/all_gather | solution.py:23
  243.8 619.4 %all-gather.7.cloned.1.call-start = ((), (), s32[]{:S(2)}) async-start(), calls=%async_computation.6 | async-start | bytes 7864320 | tf_op jit(solution)/shard_map/all_gather | solution.py:26
  244.4 707.5 %reduce-scatter.6.cloned.1.call-start = ((), (), s32[]{:S(2)}) async-start(), calls=%async_computation.5 | async-start | bytes 5242880 | tf_op jit(solution)/shard_map/reduce_scatter | solution.py:29
  429.0 1015.3 %reduce-scatter.8.cloned.1.call-start = ((), (), s32[]{:S(2)}) async-start(), calls=%async_computation.9 | async-start | bytes 35389440 | tf_op jit(solution)/shard_map/reduce_scatter | solution.py:52
  1447.5 5.8 copy-start.2
  1447.5 7.9 copy-start.1
Sparse Core Ops, SparseCore 0:
  28.4 209.9 reduce-scatter.3
  240.6 175.4 all-gather.4
  418.3 32.6 all-gather.10
  452.9 362.4 all-gather.8
  816.8 46.3 all-gather.6
  866.2 44.4 reduce-scatter.5
  950.1 494.1 reduce-scatter.7
where the time goes:
time: 1460 us
  waiting for transfers between devices  1300 us (89%)
  matrix products  80.3 us (6%)
  other arithmetic  39 us (3%)
  local copies, waits for them, and re-layouts  25.4 us (2%)
    reduce_scatter x1, waiting for transfers between devices, shards(): lax.psum_scatter(joined.reshape(blocks * stride, mcols).astype(jnp.bfloat...  486 us
    all_gather x1, waiting for transfers between devices, shards(): lax.all_gather(right_low, 'dp', axis=0, tiled=True)  364 us
    reduce_scatter x1, waiting for transfers between devices, shards(): lax.psum_scatter(lax.dot_general(inputs, out_grads, (((0,), (0,)), ((), (...  210 us
    all_gather x1, waiting for transfers between devices, shards(): lax.all_gather(summed, 'dp', axis=0, tiled=True)  172 us
    all_gather x1, waiting for transfers between devices, shards(): lax.all_gather(summed, 'tensor', axis=1, tiled=True)  47.8 us
    dot_general x1, matrix products, shards(): lax.dot_general(left_rows, turned, (((0,), (0,)), ((), ())), preferred_el...  32.4 us
  transfers between devices with their start and end apart: 7, of which 6 were waited for; matrix products, arithmetic and copies ran while one was open for 8% of the time, Pallas kernels for 0%

commit v1 on v0

--- a/solution.py
+++ b/solution.py
@@ -2,6 +2,19 @@
 import jax.numpy as jnp
 from jax import lax
 from jax.sharding import PartitionSpec as P
+
+
+def gather_around(x, axis, dim):
+    ways = lax.axis_size(axis)
+    up = [(d, (d + 1) % ways) for d in range(ways)]
+    down = [(d, (d - 1) % ways) for d in range(ways)]
+    earlier, later = ([x], [x])
+    for _ in range(ways // 2):
+        earlier.append(lax.ppermute(earlier[-1], axis, up))
+    for _ in range((ways - 1) // 2):
+        later.append(lax.ppermute(later[-1], axis, down))
+    line = jnp.concatenate([*earlier[::-1], *later[1:]], axis=dim)
+    return jnp.roll(line, (lax.axis_index(axis) - ways // 2) * x.shape[dim], axis=dim)
 
 
 def shards(inputs, out_grads, left_factor, right_factor, left_basis, right_basis):
@@ -20,7 +33,7 @@
     )
     col_panel, basis_panel = (
         lax.all_gather(summed, "dp", axis=0, tiled=True),
-        lax.all_gather(right_low, "dp", axis=0, tiled=True),
+        gather_around(right_low, "dp", 0),
     )
     row_panel, left_rows = (
         lax.all_gather(summed, "tensor", axis=1, tiled=True),

time: 1460 us -> 1370 us (0.938)
  waiting for transfers between devices: 1300 us -> 1150 us
  local copies, waits for them, and re-layouts: 25.4 us -> 61.4 us
  starting transfers between devices: 0.46 us -> 23.1 us
    ppermute x0 -> x7, waiting for transfers between devices: none -> 442 us  [the longest x4 442 us: gather_around(): earlier.append(lax.ppermute(earlier[-1], axis, up))]
    all_gather x1 -> x0, waiting for transfers between devices: 364 us -> none  [shards(): lax.all_gather(right_low, 'dp', axis=0, tiled=True)]
    all_gather x1, waiting for transfers between devices: 172 us -> 0.01 us  [shards(): lax.all_gather(summed, 'dp', axis=0, tiled=True)]
    all_gather x1, waiting for transfers between devices: 47.8 us -> 0.02 us  [shards(): lax.all_gather(summed, 'tensor', axis=1, tiled=True)]
    unnamed x12 -> x31, local copies, waits for them, and re-layouts: 6.75 us -> 42.1 us
    ppermute x0 -> x7, starting transfers between devices: none -> 22.7 us  [the longest x3 16.1 us: gather_around(): later.append(lax.ppermute(later[-1], axis, down))]
    all_gather x1, waiting for transfers between devices: 21.7 us -> 0.02 us  [shards(): lax.all_gather(left_low, 'tensor', axis=1, tiled=True)]
  transfers between devices with their start and end apart: 7 -> 13, of which waited for: 6 -> 6; matrix products, arithmetic and copies ran while one was open for 8% -> 11% of each run, Pallas kernels for 0% -> 0%
where the time goes in v1:
time: 1370 us; the launch traced here: 1360 us
  waiting for transfers between devices  1150 us (84%)
  matrix products  73.1 us (5%)
  local copies, waits for them, and re-layouts  61.4 us (4%)
  other arithmetic  44 us (3%)
  starting transfers between devices  23.1 us (2%)
  between operations  14.2 us (1%)
    reduce_scatter x1, waiting for transfers between devices, shards(): lax.psum_scatter(joined.reshape(blocks * stride, mcols).astype(jnp.bfloat...  497 us
    ppermute x4, waiting for transfers between devices, gather_around(): earlier.append(lax.ppermute(earlier[-1], axis, up))  442 us
    reduce_scatter x1, waiting for transfers between devices, shards(): lax.psum_scatter(lax.dot_general(inputs, out_grads, (((0,), (0,)), ((), (...  210 us
    unnamed x31, local copies, waits for them, and re-layouts  42.1 us
  transfers between devices with their start and end apart: 13, of which 6 were waited for; matrix products, arithmetic and copies ran while one was open for 11% of the time, Pallas kernels for 0%

profile of v1, /device:TPU:0, one launch (start us, length us, event | category | flops | bytes accessed | tf_op | source)
XLA Modules:
  0.0 1364.5 jit_solution(10536834132787965478)
XLA Ops:
  9.1 19.1 %convolution_convert_fusion.2 = bf16[4096,1536]{1,0:T(8,128)(2,1)} fusion(bf16[1024,4096]{1,0:T(8,128)(2,1)} %param.6, bf16[1024,1536]{1,0:T(8,128)(2,1)S(1)} %copy-done), kind=kOutput, calls=%fused_computation.5 | convolution fusion | flops 12891193344 | bytes 24117248 | tf_op jit(solution)/shard_map/dot_general | solution.py:27
  28.3 210.1 %reduce-scatter.4.cloned.1.call-done = bf16[512,1536]{1,0:T(8,128)(2,1)} async-done(((bf16[4096,1536]{1,0:T(8,128)(2,1)}), bf16[512,1536]{1,0:T(8,128)(2,1)}) %reduce-scatter.4.cloned.1.call-update) | async-done | bytes 1572880 | tf_op jit(solution)/shard_map/reduce_scatter | solution.py:26
  238.4 4.0 convert_element_type.28
  246.7 96.5 %collective-permute-done = bf16[768,1536]{1,0:T(8,128)(2,1)S(1)} collective-permute-done((bf16[768,1536]{1,0:T(8,128)(2,1)}, bf16[768,1536]{1,0:T(8,128)(2,1)S(1)}, u32[]{:S(2)}, u32[]{:S(2)}) %collective-permute-start) | collective-permute-done | bytes 2359328 | tf_op jit(solution)/shard_map/ppermute | solution.py:13
  343.2 4.7 collective-permute-start.4
  348.0 145.8 %collective-permute-done.1 = bf16[768,1536]{1,0:T(8,128)(2,1)S(1)} collective-permute-done((bf16[768,1536]{1,0:T(8,128)(2,1)S(1)}, bf16[768,1536]{1,0:T(8,128)(2,1)S(1)}, u32[]{:S(2)}, u32[]{:S(2)}) %collective-permute-start.1) | collective-permute-done | bytes 2359328 | tf_op jit(solution)/shard_map/ppermute | solution.py:13
  497.6 5.3 collective-permute-start.5
  503.0 108.2 %collective-permute-done.2 = bf16[768,1536]{1,0:T(8,128)(2,1)} collective-permute-done((bf16[768,1536]{1,0:T(8,128)(2,1)S(1)}, bf16[768,1536]{1,0:T(8,128)(2,1)}, u32[]{:S(2)}, u32[]{:S(2)}) %collective-permute-start.2) | collective-permute-done | bytes 2359328 | tf_op jit(solution)/shard_map/ppermute | solution.py:13
  613.9 6.1 collective-permute-start.6
  620.0 91.2 %collective-permute-done.3 = bf16[768,1536]{1,0:T(8,128)(2,1)} collective-permute-done((bf16[768,1536]{1,0:T(8,128)(2,1)}, bf16[768,1536]{1,0:T(8,128)(2,1)}, u32[]{:S(2)}, u32[]{:S(2)}) %collective-permute-start.3) | collective-permute-done | bytes 2359328 | tf_op jit(solution)/shard_map/ppermute | solution.py:13
  711.2 3.3 constant_dynamic-update-slice_fusion.15
  714.5 3.3 constant_dynamic-update-slice_fusion.14
  722.6 3.3 constant_dynamic-update-slice_fusion.10
  733.9 3.2 constant_dynamic-update-slice_fusion.6
  742.0 3.3 constant_dynamic-update-slice_fusion.2
  745.4 3.2 constant_dynamic-update-slice_fusion.1
  750.2 12.9 convolution_convert_fusion.3
  763.4 25.1 %fusion.2 = bf16[4096,1536]{0,1:T(8,128)(2,1)} fusion(bf16[512,4096]{1,0:T(8,128)(2,1)} %all-gather.8.cloned.1.call-done, bf16[512,6144]{1,0:T(8,128)(2,1)} %all-gather.6.cloned.1.call-done, bf16[12288,1536]{1,0:T(8,128)(2,1)} %constant_dynamic-update-slice_fusion, s32[]{:T(128)S(6)} %select_n.14), kind=kOutput, calls=%fused_computation.6 | convolution fusion | flops 16113205248 | bytes 41943044 | tf_op jit(solution)/shard_map/dot_general | solution.py:59
  788.5 15.7 %copy.12 = bf16[4096,1536]{1,0:T(8,128)(2,1)} copy(bf16[4096,1536]{0,1:T(8,128)(2,1)} %fusion.2) | data formatting | bytes 25165824 | tf_op jit(solution)/shard_map/reshape | solution.py:63
  804.2 16.0 %convolution_convert_fusion = bf16[6144,1536]{1,0:T(8,128)(2,1)} fusion(bf16[512,6144]{1,0:T(8,128)(2,1)} %all-gather.6.cloned.1.call-done, bf16[512,1536]{1,0:T(8,128)(2,1)S(1)} %copy-done.5), kind=kOutput, calls=%fused_computation.1 | convolution fusion | flops 9673113600 | bytes 26738688 | tf_op jit(solution)/shard_map/dot_general | solution.py:56
  820.2 21.8 %pad_maximum_fusion = bf16[8,1280,1536]{2,1,0:T(8,128)(2,1)} fusion(bf16[8,512,1536]{2,1,0:T(8,128)(2,1)} %bitcast.16, bf16[8,768,1536]{2,1,0:T(8,128)(2,1)} %bitcast.19), kind=kLoop, calls=%fused_computation | loop fusion | flops 62914560 | bytes 62914560 | tf_op jit(solution)/shard_map/concatenate | solution.py:62
  849.8 496.6 %reduce-scatter.8.cloned.1.call-done = bf16[1280,1536]{1,0:T(8,128)(2,1)} async-done(((bf16[10240,1536]{1,0:T(8,128)(2,1)}), bf16[1280,1536]{1,0:T(8,128)(2,1)}) %reduce-scatter.8.cloned.1.call-update) | async-done | bytes 3932176 | tf_op jit(solution)/shard_map/reduce_scatter | solution.py:65
  1346.4 3.3 convert_element_type.32
  1349.7 5.8 fusion.3
  (55 shorter events, 42.3 us)
Async XLA Ops:
  7.2 1.9 copy-start
  7.2 231.2 %reduce-scatter.4.cloned.1.call-start = ((), (), s32[]{:S(2)}) async-start(), calls=%async_computation.3 | async-start | bytes 14155776 | tf_op jit(solution)/shard_map/reduce_scatter | solution.py:26
  28.2 722.0 %all-gather.4.cloned.1.call-start = ((), (), s32[]{:S(2)}) async-start(), calls=%async_computation.4 | async-start | bytes 14155776 | tf_op jit(solution)/shard_map/all_gather | solution.py:35
  238.4 525.0 %all-gather.8.cloned.1.call-start = ((), (), s32[]{:S(2)}) async-start(), calls=%async_computation.7 | async-start | bytes 5242880 | tf_op jit(solution)/shard_map/all_gather | solution.py:40
  242.4 100.8 %collective-permute-start = (bf16[768,1536]{1,0:T(8,128)(2,1)}, bf16[768,1536]{1,0:T(8,128)(2,1)S(1)}, u32[]{:S(2)}, u32[]{:S(2)}) collective-permute-start(bf16[768,1536]{1,0:T(8,128)(2,1)} %convert_element_type.28), channel_id=1, source_target_pairs={{0,4},{4,8},{8,12},{12,16},{16,20},{20,24},{24,28},{28,0},{1,5},{5... | collective-permute-start | bytes 7077896 | tf_op jit(solution)/shard_map/ppermute | solution.py:13
  246.6 516.8 %all-gather.6.cloned.1.call-start = ((), (), s32[]{:S(2)}) async-start(), calls=%async_computation.6 | async-start | bytes 7864320 | tf_op jit(solution)/shard_map/all_gather | solution.py:39
  343.2 150.5 %collective-permute-start.1 = (bf16[768,1536]{1,0:T(8,128)(2,1)S(1)}, bf16[768,1536]{1,0:T(8,128)(2,1)S(1)}, u32[]{:S(2)}, u32[]{:S(2)}) collective-permute-start(bf16[768,1536]{1,0:T(8,128)(2,1)S(1)} %collective-permute-done), channel_id=1, source_target_pairs={{0,4},{4,8},{8,12},{12,16},{16,20},{20,24},{24,28},{28,0},{1,5},{5... | collective-permute-start | bytes 7077896 | tf_op jit(solution)/shard_map/ppermute | solution.py:13
  343.2 154.4 %collective-permute-start.4 = (bf16[768,1536]{1,0:T(8,128)(2,1)}, bf16[768,1536]{1,0:T(8,128)(2,1)}, u32[]{:S(2)}, u32[]{:S(2)}) collective-permute-start(bf16[768,1536]{1,0:T(8,128)(2,1)} %convert_element_type.28), channel_id=1, source_target_pairs={{0,28},{4,0},{8,4},{12,8},{16,12},{20,16},{24,20},{28,24},{1,29},{... | collective-permute-start | bytes 7077896 | tf_op jit(solution)/shard_map/ppermute | solution.py:15
  493.7 1.4 copy-start.3
  495.1 116.0 %collective-permute-start.2 = (bf16[768,1536]{1,0:T(8,128)(2,1)S(1)}, bf16[768,1536]{1,0:T(8,128)(2,1)}, u32[]{:S(2)}, u32[]{:S(2)}) collective-permute-start(bf16[768,1536]{1,0:T(8,128)(2,1)S(1)} %collective-permute-done.1), channel_id=1, source_target_pairs={{0,4},{4,8},{8,12},{12,16},{16,20},{20,24},{24,28},{28,0},{1,5},{5... | collective-permute-start | bytes 7077896 | tf_op jit(solution)/shard_map/ppermute | solution.py:13
  497.6 116.3 %collective-permute-start.5 = (bf16[768,1536]{1,0:T(8,128)(2,1)}, bf16[768,1536]{1,0:T(8,128)(2,1)}, u32[]{:S(2)}, u32[]{:S(2)}) collective-permute-start(bf16[768,1536]{1,0:T(8,128)(2,1)} %collective-permute-done.4), channel_id=1, source_target_pairs={{0,28},{4,0},{8,4},{12,8},{16,12},{20,16},{24,20},{28,24},{1,29},{... | collective-permute-start | bytes 7077896 | tf_op jit(solution)/shard_map/ppermute | solution.py:15
  611.2 100.0 %collective-permute-start.3 = (bf16[768,1536]{1,0:T(8,128)(2,1)}, bf16[768,1536]{1,0:T(8,128)(2,1)}, u32[]{:S(2)}, u32[]{:S(2)}) collective-permute-start(bf16[768,1536]{1,0:T(8,128)(2,1)} %collective-permute-done.2), channel_id=1, source_target_pairs={{0,4},{4,8},{8,12},{12,16},{16,20},{20,24},{24,28},{28,0},{1,5},{5... | collective-permute-start | bytes 7077896 | tf_op jit(solution)/shard_map/ppermute | solution.py:13
  613.8 230.2 %reduce-scatter.6.cloned.1.call-start = ((), (), s32[]{:S(2)}) async-start(), calls=%async_computation.5 | async-start | bytes 5242880 | tf_op jit(solution)/shard_map/reduce_scatter | solution.py:42
  613.9 103.8 %copy-start.4 = (bf16[768,1536]{1,0:T(8,128)(2,1)S(1)}, bf16[768,1536]{1,0:T(8,128)(2,1)}, u32[]{:S(2)}) copy-start(bf16[768,1536]{1,0:T(8,128)(2,1)} %copy-done.3) | copy-start | bytes 7077892
  613.9 107.1 %slice-start = ((s8[4718592]{0:T(1024)(128)(4,1)}), s8[4194304]{0:T(1024)(128)(4,1)S(1)}, s32[]{:S(2)}) async-start(s8[4718592]{0:T(1024)(128)(4,1)} %bitcast.17), calls=%async_computation.9 | async-start | bytes 8388608
  613.9 115.2 %collective-permute-start.6 = (bf16[768,1536]{1,0:T(8,128)(2,1)}, bf16[768,1536]{1,0:T(8,128)(2,1)S(1)}, u32[]{:S(2)}, u32[]{:S(2)}) collective-permute-start(bf16[768,1536]{1,0:T(8,128)(2,1)} %collective-permute-done.5), channel_id=1, source_target_pairs={{0,28},{4,0},{8,4},{12,8},{16,12},{20,16},{24,20},{28,24},{1,29},{... | collective-permute-start | bytes 7077896 | tf_op jit(solution)/shard_map/ppermute | solution.py:15
  717.7 3.2 slice-start.1
  742.0 8.2 copy-start.5
  763.1 583.3 %reduce-scatter.8.cloned.1.call-start = ((), (), s32[]{:S(2)}) async-start(), calls=%async_computation.8 | async-start | bytes 35389440 | tf_op jit(solution)/shard_map/reduce_scatter | solution.py:65
  1346.4 11.2 copy-start.1
  1349.7 5.8 copy-start.2
Sparse Core Ops, SparseCore 0:
  28.3 209.9 reduce-scatter.3
  240.5 379.1 all-gather.3
  621.9 35.8 all-gather.7
  659.1 46.3 all-gather.5
  763.2 53.4 reduce-scatter.5
  842.2 504.1 reduce-scatter.7
